TPU v7x, 128 devices: a whole 4x4x4 slice. The times are simulated.
128 devices in a mesh: fsdp: 16 (over z_hi, y, core), ctx: 8 (over z_lo, x).
Axes of the slice: x: 4, y: 4, z: 4 (z_hi: 2, z_lo: 2; z = z_hi * 2 + z_lo), core: 2. Of those that a mesh axis runs over, the one named last changes fastest.
Arguments:
- tokens: bfloat16 [16, 2048, 1024], P('fsdp', 'ctx'), may hold values from -6 to 6
- first_value: bfloat16 [16, 2048, 1024], P('fsdp', 'ctx'), may hold values from -6 to 6
- query_weight: bfloat16 [1024, 1024], P('fsdp'), may hold values from -0.1875 to 0.1875
- key_weight: bfloat16 [1024, 1024], P('fsdp'), may hold values from -0.1875 to 0.1875
- value_weight: bfloat16 [1024, 1024], P('fsdp'), may hold values from -0.1875 to 0.1875
- out_weight: bfloat16 [1024, 1024], P('fsdp'), may hold values from -1.5 to 1.5
- gate_weight: bfloat16 [1024, 2816], P('fsdp'), may hold values from -0.1875 to 0.1875
- up_weight: bfloat16 [1024, 2816], P('fsdp'), may hold values from -0.1875 to 0.1875
- down_weight: bfloat16 [2816, 1024], P('fsdp'), may hold values from -0.109375 to 0.109375
- prenorm_gain: bfloat16 [1024], P('fsdp'), may hold values from 0.5 to 1.5
- midnorm_gain: bfloat16 [1024], P('fsdp'), may hold values from 0.5 to 1.5
- cotangent: bfloat16 [16, 2048, 1024], P('fsdp', 'ctx'), may hold values from -6 to 6
- lengths: int32 [16], replicated, may hold values from 1 to 2048, 22528 in all
- assignment: int32 [16], replicated, may hold values from 0 to 15, each once
Outputs:
- layer_out: bfloat16 [16, 2048, 1024], P('fsdp', 'ctx')
- tokens_grad: float32 [16, 2048, 1024], P('fsdp', 'ctx')
- first_grad: float32 [16, 2048, 1024], P('fsdp', 'ctx')
- query_grad: float32 [1024, 1024], P('fsdp')
- key_grad: float32 [1024, 1024], P('fsdp')
- value_grad: float32 [1024, 1024], P('fsdp')
- out_grad: float32 [1024, 1024], P('fsdp')
- gate_grad: float32 [1024, 2816], P('fsdp')
- up_grad: float32 [1024, 2816], P('fsdp')
- down_grad: float32 [2816, 1024], P('fsdp')
- prenorm_grad: float32 [1024], P('fsdp')
- midnorm_grad: float32 [1024], P('fsdp')
Inputs may be any that keep to these rules, and one draw needn't show every extreme that they name: lengths of the sequences sum to 22528; the longest is exactly 2048. `assignment`: each sequence stands in exactly one slot.
All inputs are finite; a program needn't handle non-finite values.
Results may differ from a plain program's by a relative error of at most 0.025.
Values may be sent and summed in bfloat16 or wider, within the bound.
No kernel may reach another device: no remote copies, remote signals or barrier semaphores. Data moves between devices by JAX's collectives and lax.ppermute only.
A program may use at most 256 MiB of HBM per device.

v0:
```python
import math
import jax
import jax.numpy as jnp
from jax import lax
from jax.sharding import PartitionSpec as P

H = 16
EPS = 1e-06
MASKED = -1e30
GAIN_ROWS = 16


def rope_tables(positions, half):
    freq = jnp.exp(
        jnp.arange(half, dtype=jnp.int32).astype(jnp.float32) * (-math.log(10000.0) / half)
    )
    angle = positions.astype(jnp.float32)[:, None] * freq[None, :]
    return (jnp.cos(angle), jnp.sin(angle))


def rotate(value_rows, cosine, sine):
    half = value_rows.shape[-1] // 2
    first = value_rows[..., :half]
    second = value_rows[..., half:]
    return jnp.concatenate(
        [first * cosine - second * sine, second * cosine + first * sine], axis=-1
    )


def norm_apply(value_rows, gain):
    inverse = lax.rsqrt(jnp.mean(value_rows * value_rows, axis=-1, keepdims=True) + EPS)
    return (value_rows * inverse * gain, inverse)


def norm_back(value_rows, inverse, gain, upstream):
    scaled = upstream * gain
    gain_part = jnp.sum(upstream * value_rows * inverse, axis=(0, 1))
    inner = jnp.mean(scaled * value_rows, axis=-1, keepdims=True)
    return (inverse * scaled - value_rows * inverse * inverse * inverse * inner, gain_part)


def gain_block(first, second, width, leading=()):
    pad_cols = width - first.shape[-1] - second.shape[-1]
    row = jnp.concatenate([first, second, jnp.zeros(leading + (pad_cols,), first.dtype)], axis=-1)
    row = row[..., None, :]
    pads = [(0, 0)] * len(leading) + [(0, GAIN_ROWS - 1), (0, 0)]
    return jnp.pad(row, pads)


def body(
    tokens,
    first_value,
    query_weight,
    key_weight,
    value_weight,
    out_weight,
    gate_weight,
    up_weight,
    down_weight,
    prenorm_gain,
    midnorm_gain,
    cotangent,
    lengths,
    assignment,
):
    slots, rows, width = tokens.shape
    head_count = H
    head_dim = width // head_count
    score_scale = head_dim ** (-0.5)
    n_fsdp = lax.axis_size("fsdp")
    n_ctx = lax.axis_size("ctx")
    total_len = rows * n_ctx
    w_rows = query_weight.shape[0]
    g_len = prenorm_gain.shape[0]
    ff = gate_weight.shape[1]
    d_rows = down_weight.shape[0]
    slot_count = assignment.shape[0]
    chosen = assignment[:, None] == jnp.arange(slot_count, dtype=jnp.int32)[None, :]
    lengths_all = jnp.sum(jnp.where(chosen, lengths[None, :], 0), axis=1)
    slot_lengths = lax.dynamic_slice_in_dim(lengths_all, lax.axis_index("fsdp") * slots, slots)
    query_places = lax.axis_index("ctx") * rows + jnp.arange(rows, dtype=jnp.int32)
    key_places = jnp.arange(total_len, dtype=jnp.int32)
    valid = query_places[None, :] < slot_lengths[:, None]
    allowed = (key_places[None, None, :] <= query_places[None, :, None]) & (
        key_places[None, None, :] < slot_lengths[:, None, None]
    )
    cosine, sine = rope_tables(query_places, head_dim // 2)
    cos_rows = cosine[None, :, None, :]
    sin_rows = sine[None, :, None, :]
    valid_wide = valid[:, :, None]
    attn_pack = jnp.concatenate(
        [
            query_weight,
            key_weight,
            value_weight,
            out_weight,
            gain_block(prenorm_gain, midnorm_gain, width),
        ],
        axis=0,
    )
    attn_all = lax.all_gather(attn_pack, "fsdp", axis=0, tiled=False)

    def attn_part(i):
        return attn_all[:, i * w_rows : (i + 1) * w_rows, :].reshape(n_fsdp * w_rows, width)

    query_mat, key_mat, value_mat, out_mat = (attn_part(i) for i in range(4))
    prenorm_full = attn_all[:, 4 * w_rows, 0:g_len].reshape(n_fsdp * g_len)
    midnorm_full = attn_all[:, 4 * w_rows, g_len : 2 * g_len].reshape(n_fsdp * g_len)
    mlp_pack = jnp.concatenate([gate_weight, up_weight, down_weight.reshape(w_rows, ff)], axis=1)
    mlp_all = lax.all_gather(mlp_pack, "fsdp", axis=0, tiled=False)
    gate_mat = mlp_all[:, :, 0:ff].reshape(n_fsdp * w_rows, ff)
    upper_mat = mlp_all[:, :, ff : 2 * ff].reshape(n_fsdp * w_rows, ff)
    down_mat = (
        mlp_all[:, :, 2 * ff :].reshape(n_fsdp, d_rows, width).reshape(n_fsdp * d_rows, width)
    )
    tokens_wide = tokens.astype(jnp.float32)
    first_wide = first_value.astype(jnp.float32)
    normed, inverse = norm_apply(tokens_wide, prenorm_full.astype(jnp.float32))
    normed_low = normed.astype(jnp.bfloat16)
    query = jnp.dot(normed_low, query_mat, preferred_element_type=jnp.float32)
    keyed = jnp.dot(normed_low, key_mat, preferred_element_type=jnp.float32)
    own_value = jnp.dot(normed_low, value_mat, preferred_element_type=jnp.float32)
    heads_shape = query.shape[:2] + (head_count, head_dim)
    query_rotated_rows = rotate(query.reshape(heads_shape), cos_rows, sin_rows).astype(jnp.bfloat16)
    key_rot = (
        rotate(keyed.reshape(heads_shape), cos_rows, sin_rows)
        .astype(jnp.bfloat16)
        .reshape(query.shape)
    )
    value_mix = (0.5 * own_value + 0.5 * first_wide).astype(jnp.bfloat16)
    kv_all = lax.all_gather(
        jnp.concatenate([key_rot, value_mix], axis=-1), "ctx", axis=1, tiled=True
    )
    key_rows_per_head = kv_all[..., :width].reshape(slots, total_len, head_count, head_dim)
    value_rows_per_head = kv_all[..., width:].reshape(slots, total_len, head_count, head_dim)
    scores = (
        jnp.einsum(
            "biuv,bfuv->buif",
            query_rotated_rows,
            key_rows_per_head,
            preferred_element_type=jnp.float32,
        )
        * score_scale
    )
    scores = jnp.where(allowed[:, None], scores, MASKED)
    peak = jnp.max(scores, axis=-1, keepdims=True)
    raised = jnp.exp(scores - peak)
    denominator = jnp.sum(raised, axis=-1, keepdims=True)
    shares = raised / denominator
    attention_share_narrow = shares.astype(jnp.bfloat16)
    mixed = jnp.einsum(
        "ytjo,yotv->yjtv",
        attention_share_narrow,
        value_rows_per_head,
        preferred_element_type=jnp.float32,
    )
    mixed_low = mixed.astype(jnp.bfloat16).reshape(slots, rows, width)
    middle = tokens_wide + jnp.dot(mixed_low, out_mat, preferred_element_type=jnp.float32)
    normed_two, inverse_two = norm_apply(middle, midnorm_full.astype(jnp.float32))
    normed_two = normed_two.astype(jnp.bfloat16)
    gate = jnp.dot(normed_two, gate_mat, preferred_element_type=jnp.float32)
    upper = jnp.dot(normed_two, upper_mat, preferred_element_type=jnp.float32)
    hidden = (jax.nn.silu(gate) * upper).astype(jnp.bfloat16)
    branch = jnp.dot(hidden, down_mat, preferred_element_type=jnp.float32)
    layer_out = jnp.where(valid_wide, middle + branch, 0.0).astype(jnp.bfloat16)
    cot_wide = jnp.where(valid_wide, cotangent.astype(jnp.float32), 0.0)
    cot_low = cot_wide.astype(jnp.bfloat16)
    down_total = jnp.einsum("srf,sre->fe", hidden, cot_low, preferred_element_type=jnp.float32)
    hidden_back = jnp.einsum("sre,fe->srf", cot_low, down_mat, preferred_element_type=jnp.float32)
    sigma = jax.nn.sigmoid(gate)
    gate_back = (hidden_back * upper * sigma * (1.0 + gate * (1.0 - sigma))).astype(jnp.bfloat16)
    upper_back = (hidden_back * gate * sigma).astype(jnp.bfloat16)
    gate_total = jnp.einsum(
        "srd,srf->df", normed_two, gate_back, preferred_element_type=jnp.float32
    )
    upper_total = jnp.einsum(
        "srd,srf->df", normed_two, upper_back, preferred_element_type=jnp.float32
    )
    normed_two_back = jnp.einsum(
        "srf,df->srd", gate_back, gate_mat, preferred_element_type=jnp.float32
    )
    normed_two_back = normed_two_back + jnp.einsum(
        "srf,df->srd", upper_back, upper_mat, preferred_element_type=jnp.float32
    )
    middle_norm_back, midnorm_total = norm_back(
        middle, inverse_two, midnorm_full.astype(jnp.float32), normed_two_back
    )
    middle_back = cot_wide + middle_norm_back
    middle_low = middle_back.astype(jnp.bfloat16)
    out_total = jnp.einsum("srd,sre->de", mixed_low, middle_low, preferred_element_type=jnp.float32)
    mlp_grads = jnp.concatenate(
        [
            gate_total.reshape(n_fsdp, w_rows, ff),
            upper_total.reshape(n_fsdp, w_rows, ff),
            down_total.reshape(n_fsdp, d_rows, width).reshape(n_fsdp, w_rows, ff),
            out_total.reshape(n_fsdp, w_rows, width),
        ],
        axis=2,
    ).astype(jnp.bfloat16)
    mlp_share = lax.psum_scatter(mlp_grads, "fsdp", scatter_dimension=0, tiled=False)
    blended_value_gradient = jnp.einsum(
        "sre,de->srd", middle_low, out_mat, preferred_element_type=jnp.float32
    ).astype(jnp.bfloat16)
    blended_value_gradient = blended_value_gradient.reshape(slots, rows, head_count, head_dim)
    prob_back = jnp.einsum(
        "biuv,bfuv->buif",
        blended_value_gradient,
        value_rows_per_head,
        preferred_element_type=jnp.float32,
    )
    inner = jnp.sum(shares * prob_back, axis=-1, keepdims=True)
    score_gradient = (shares * (prob_back - inner)).astype(jnp.bfloat16)
    query_rot_back = (
        jnp.einsum(
            "ytjo,yotv->yjtv", score_gradient, key_rows_per_head, preferred_element_type=jnp.float32
        )
        * score_scale
    )
    key_part = (
        jnp.einsum(
            "xtfk,xfty->kxty",
            score_gradient,
            query_rotated_rows,
            preferred_element_type=jnp.float32,
        )
        * score_scale
    )
    value_part = jnp.einsum(
        "xtfk,xfty->kxty",
        attention_share_narrow,
        blended_value_gradient,
        preferred_element_type=jnp.float32,
    )
    key_value = lax.psum_scatter(
        jnp.concatenate(
            [
                key_part.reshape(total_len, slots, width),
                value_part.reshape(total_len, slots, width),
            ],
            axis=-1,
        ).astype(jnp.bfloat16),
        "ctx",
        scatter_dimension=0,
        tiled=True,
    ).astype(jnp.float32)
    key_value = jnp.swapaxes(key_value, 0, 1)
    key_rot_back = key_value[..., :width].reshape(slots, rows, head_count, head_dim)
    value_mix_back = key_value[..., width:]
    first_grad = 0.5 * value_mix_back
    query_back = (
        rotate(query_rot_back, cos_rows, -sin_rows).reshape(slots, rows, width).astype(jnp.bfloat16)
    )
    key_back = (
        rotate(key_rot_back, cos_rows, -sin_rows).reshape(slots, rows, width).astype(jnp.bfloat16)
    )
    value_back = (0.5 * value_mix_back).astype(jnp.bfloat16)
    query_total = jnp.einsum(
        "srd,sre->de", normed_low, query_back, preferred_element_type=jnp.float32
    )
    key_total = jnp.einsum("srd,sre->de", normed_low, key_back, preferred_element_type=jnp.float32)
    value_total = jnp.einsum(
        "srd,sre->de", normed_low, value_back, preferred_element_type=jnp.float32
    )
    normed_back = jnp.einsum(
        "sre,de->srd", query_back, query_mat, preferred_element_type=jnp.float32
    )
    normed_back = normed_back + jnp.einsum(
        "sre,de->srd", key_back, key_mat, preferred_element_type=jnp.float32
    )
    normed_back = normed_back + jnp.einsum(
        "sre,de->srd", value_back, value_mat, preferred_element_type=jnp.float32
    )
    tokens_norm_back, prenorm_total = norm_back(
        tokens_wide, inverse, prenorm_full.astype(jnp.float32), normed_back
    )
    tokens_grad = middle_back + tokens_norm_back
    attn_grads = jnp.concatenate(
        [
            query_total.reshape(n_fsdp, w_rows, width),
            key_total.reshape(n_fsdp, w_rows, width),
            value_total.reshape(n_fsdp, w_rows, width),
            gain_block(
                prenorm_total.reshape(n_fsdp, g_len),
                midnorm_total.reshape(n_fsdp, g_len),
                width,
                leading=(n_fsdp,),
            ),
        ],
        axis=1,
    ).astype(jnp.bfloat16)
    attn_share = lax.psum_scatter(attn_grads, "fsdp", scatter_dimension=0, tiled=False)
    attn_share, mlp_share = lax.psum((attn_share, mlp_share), "ctx")
    attn_share = attn_share.astype(jnp.float32)
    mlp_share = mlp_share.astype(jnp.float32)

    def attn_grad(i):
        return attn_share[i * w_rows : (i + 1) * w_rows]

    query_grad, key_grad, value_grad = (attn_grad(i) for i in range(3))
    prenorm_grad = attn_share[3 * w_rows, 0:g_len]
    midnorm_grad = attn_share[3 * w_rows, g_len : 2 * g_len]
    gate_grad = mlp_share[:, 0:ff]
    up_grad = mlp_share[:, ff : 2 * ff]
    down_grad = mlp_share[:, 2 * ff : 3 * ff].reshape(d_rows, width)
    out_grad = mlp_share[:, 3 * ff :]
    return (
        layer_out,
        tokens_grad,
        first_grad,
        query_grad,
        key_grad,
        value_grad,
        out_grad,
        gate_grad,
        up_grad,
        down_grad,
        prenorm_grad,
        midnorm_grad,
    )


def solution(mesh):
    placed = (
        P("fsdp", "ctx", None),
        P("fsdp", "ctx", None),
        P("fsdp", None),
        P("fsdp", None),
        P("fsdp", None),
        P("fsdp", None),
        P("fsdp", None),
        P("fsdp", None),
        P("fsdp", None),
        P("fsdp"),
        P("fsdp"),
        P("fsdp", "ctx", None),
        P(),
        P(),
    )
    return jax.shard_map(
        body,
        mesh=mesh,
        in_specs=placed,
        out_specs=(
            P("fsdp", "ctx", None),
            P("fsdp", "ctx", None),
            P("fsdp", "ctx", None),
            P("fsdp", None),
            P("fsdp", None),
            P("fsdp", None),
            P("fsdp", None),
            P("fsdp", None),
            P("fsdp", None),
            P("fsdp", None),
            P("fsdp"),
            P("fsdp"),
        ),
        check_vma=False,
    )
```

profile of v0, /device:TPU:0, one launch (start us, length us, event | category | flops | bytes accessed | tf_op | source)
XLA Modules:
  0.0 923.7 jit_solution(8580043544185926141)
XLA Ops:
  15.1 75.5 %all-gather.8.cloned.1.call-done = bf16[4352,1024]{1,0:T(8,128)(2,1)} async-done(((bf16[272,1024]{1,0:T(8,128)(2,1)}), bf16[4352,1024]{1,0:T(8,128)(2,1)}) %all-gather.8.cloned.1.call-update) | async-done | bytes 8912912 | tf_op jit(solution)/shard_map/all_gather | solution.py:101
  91.6 5.8 fusion.81
  122.6 84.4 %all-gather.6.cloned.1.call-done = bf16[1,2048,2048]{2,1,0:T(8,128)(2,1)} async-done(((bf16[1,256,2048]{2,1,0:T(8,128)(2,1)}), bf16[1,2048,2048]{2,1,0:T(8,128)(2,1)}) %all-gather.6.cloned.1.call-update) | async-done | bytes 8388624 | tf_op jit(solution)/shard_map/all_gather | solution.py:131
  207.0 6.4 fusion.82
  213.4 6.6 copy.63
  220.0 6.7 copy.61
  226.6 15.6 %fusion.55 = f32[16,256,2048]{2,1,0:T(8,128)} fusion(bf16[2048,16,64]{0,2,1:T(8,128)(2,1)} %bitcast.190, bf16[256,16,32]{0,2,1:T(8,128)(2,1)S(1)} %get-tuple-element.42, bf16[256,16,32]{0,2,1:T(8,128)(2,1)S(1)} %get-tuple-element.41), kind=kOutput, calls=%fused_computation.109 | convolution fusion | flops 1074790400 | bytes 38273024 | tf_op jit(solution)/shard_map/biuv,bfuv->buif/dot_general | solution.py:137
  242.2 38.3 %fusion.86 = (f32[16,256]{1,0:T(8,128)S(1)}, f32[16,256,2048]{2,1,0:T(8,128)}) fusion(f32[16,256,2048]{2,1,0:T(8,128)} %fusion.55, pred[256,2048]{1,0:T(8,128)(4,1)S(1)} %fusion.14), kind=kOutput, calls=%fused_computation.157 | output fusion | flops 50333696 | bytes 67649536 | tf_op jit(solution)/shard_map/sub | solution.py:147
  280.5 15.9 %fusion.24 = bf16[16,64,256]{2,1,0:T(8,128)(2,1)} fusion(bf16[2048,16,64]{0,2,1:T(8,128)(2,1)} %bitcast.224, f32[16,256,2048]{2,1,0:T(8,128)} %get-tuple-element.61, f32[16,256]{1,0:T(8,128)S(1)} %get-tuple-element.60), kind=kOutput, calls=%fused_computation.57 | convolution fusion | flops 1090781184 | bytes 38289408 | tf_op jit(solution)/shard_map/ytjo,yotv->yjtv/dot_general | solution.py:151
  298.4 22.5 %all-gather.10.cloned.1.call-done = bf16[1024,8448]{1,0:T(8,128)(2,1)} async-done(((bf16[64,8448]{1,0:T(8,128)(2,1)}), bf16[1024,8448]{1,0:T(8,128)(2,1)}) %all-gather.10.cloned.1.call-update) | async-done | bytes 17301520 | tf_op jit(solution)/shard_map/all_gather | solution.py:110
  321.0 11.3 %fusion.80 = (bf16[16,64,2816]{2,1,0:T(8,128)(2,1)}, bf16[16,64,2816]{2,1,0:T(8,128)(2,1)}, bf16[16,64,2816]{2,1,0:T(8,128)(2,1)}) fusion(bf16[16,64,8448]{2,1,0:T(8,128)(2,1)} %bitcast.201), kind=kLoop, calls=%fused_computation.151 | loop fusion | bytes 34603008 | tf_op jit(solution)/shard_map/slice | solution.py:114
  332.2 12.1 %reshape_reshape.7 = bf16[2816,1024]{1,0:T(8,128)(2,1)} reshape(bf16[16,64,2816]{2,1,0:T(8,128)(2,1)} %get-tuple-element.20) | data formatting | bytes 11534336 | tf_op jit(solution)/shard_map/reshape;reshape | solution.py:114
  344.4 6.1 fusion.48
  353.8 7.5 multiply_convert_fusion.2
  367.3 14.3 %fusion.11 = bf16[16,64,2048]{2,1,0:T(8,128)(2,1)} fusion(bf16[256,16,64]{0,2,1:T(8,128)(2,1)S(1)} %bitcast.232, f32[16,256,2048]{2,1,0:T(8,128)} %get-tuple-element.61, f32[16,256]{1,0:T(8,128)S(1)} %get-tuple-element.60), kind=kOutput, calls=%fused_computation.23 | convolution fusion | flops 1092616192 | bytes 38289408 | tf_op jit(solution)/shard_map/xtfk,xfty->kxty/dot_general | solution.py:228
  381.7 22.7 %multiply_reduce_fusion = (f32[16,256]{1,0:T(8,128)S(1)}, f32[16,256,2048]{2,1,0:T(8,128)}) fusion(f32[16,256,2048]{2,1,0:T(8,128)} %get-tuple-element.61, f32[16,256]{1,0:T(8,128)S(1)} %get-tuple-element.60, bf16[256,16,64]{0,2,1:T(8,128)(2,1)S(1)} %bitcast.233, bf16[2048,16,64]{0,2,1:T(8,128)(2,1)} %bitcast.225), kind=kOutput, calls=%fused_computation.2 | convolution fusion | flops 1098903552 | bytes 71860224 | tf_op jit(solution)/shard_map/biuv,bfuv->buif/dot_general | solution.py:205
  404.4 6.4 copy.66
  410.8 27.7 %multiply_convert_fusion = bf16[16,256,2048]{2,1,0:T(8,128)(2,1)} fusion(f32[16,256,2048]{2,1,0:T(8,128)} %get-tuple-element.66, f32[16,256]{1,0:T(8,128)S(1)} %get-tuple-element.65, f32[16,256,2048]{2,1,0:T(8,128)} %get-tuple-element.61, f32[16,256]{1,0:T(8,128)S(1)} %get-tuple-element.60), kind=kLoop, calls=%fused_computation.1 | loop fusion | flops 33554432 | bytes 83918848 | tf_op jit(solution)/shard_map/convert_element_type | solution.py:212
  438.5 10.8 %multiply_convert_fusion.1 = bf16[16,64,2048]{2,1,0:T(8,128)(2,1)} fusion(bf16[16,256,2048]{2,1,0:T(8,128)(2,1)} %multiply_convert_fusion, bf16[256,16,32]{0,2,1:T(8,128)(2,1)S(1)} %copy-done.24, bf16[256,16,32]{0,2,1:T(8,128)(2,1)S(1)} %copy-done.22), kind=kOutput, calls=%fused_computation.14 | convolution fusion | flops 1078984704 | bytes 21495808 | tf_op jit(solution)/shard_map/xtfk,xfty->kxty/dot_general | solution.py:220
  449.3 6.4 copy.65
  455.8 8.2 pad_maximum_fusion.1
  464.2 13.9 %fusion.17 = f32[1,256,16,64]{1,3,2,0:T(8,128)} fusion(bf16[2048,16,64]{0,2,1:T(8,128)(2,1)} %bitcast.191, bf16[16,256,2048]{2,1,0:T(8,128)(2,1)} %multiply_convert_fusion), kind=kOutput, calls=%fused_computation.46 | convolution fusion | flops 1074003968 | bytes 22020096 | tf_op jit(solution)/shard_map/ytjo,yotv->yjtv/dot_general | solution.py:214
  478.1 76.3 %reduce-scatter.4.cloned.1.call-done = bf16[256,1,2048]{2,0,1:T(8,128)(2,1)} async-done(((bf16[2048,1,2048]{2,0,1:T(8,128)(2,1)}), bf16[256,1,2048]{2,0,1:T(8,128)(2,1)}) %reduce-scatter.4.cloned.1.call-update) | async-done | bytes 1048592 | tf_op jit(solution)/shard_map/reduce_scatter | solution.py:234
  576.0 5.4 convolution_convert_fusion
  581.4 12.1 %reshape_reshape.8 = bf16[16,64,2816]{2,1,0:T(8,128)(2,1)} reshape(bf16[2816,1024]{1,0:T(8,128)(2,1)} %convolution_convert_fusion) | data formatting | bytes 11534336 | tf_op jit(solution)/shard_map/reshape;reshape | solution.py:195
  596.8 4.2 convolution_convert_fusion.1
  601.0 5.4 convolution_convert_fusion.2
  606.4 13.3 %pad_maximum_fusion = bf16[16,64,9472]{2,1,0:T(8,128)(2,1)} fusion(bf16[16,64,1024]{2,1,0:T(8,128)(2,1)} %convolution_convert_fusion.3, bf16[16,64,2816]{2,1,0:T(8,128)(2,1)S(1)} %bitcast.194, bf16[16,64,2816]{2,1,0:T(8,128)(2,1)} %convolution_convert_fusion.1, bf16[16,64,2816]{2,1,0:T(8,128)(2,1)} %convolution_convert_fusion.2), kind=kLoop, calls=%fused_computation.6 | loop fusion | flops 77594624 | bytes 38797312 | tf_op jit(solution)/shard_map/concatenate | solution.py:191
  619.7 43.7 %reduce-scatter.6.cloned.1.call-done = bf16[1,208,1024]{2,1,0:T(8,128)(2,1)} async-done(((bf16[16,208,1024]{2,1,0:T(8,128)(2,1)}), bf16[1,208,1024]{2,1,0:T(8,128)(2,1)}) %reduce-scatter.6.cloned.1.call-update) | async-done | bytes 426000 | tf_op jit(solution)/shard_map/reduce_scatter | solution.py:291
  663.4 165.2 %reduce-scatter.8.cloned.1.call-done = bf16[1,64,9472]{2,1,0:T(8,128)(2,1)} async-done(((bf16[16,64,9472]{2,1,0:T(8,128)(2,1)}), bf16[1,64,9472]{2,1,0:T(8,128)(2,1)}) %reduce-scatter.8.cloned.1.call-update) | async-done | bytes 1212432 | tf_op jit(solution)/shard_map/reduce_scatter | solution.py:200
  828.6 5.7 fusion.23
  835.6 73.4 %all-reduce.5.cloned.1.call-done = (bf16[208,1024]{1,0:T(8,128)(2,1)}, bf16[64,9472]{1,0:T(8,128)(2,1)}) async-done(((bf16[208,1024]{1,0:T(8,128)(2,1)}, bf16[64,9472]{1,0:T(8,128)(2,1)}), (bf16[208,1024]{1,0:T(8,128)(2,1)}, bf16[64,9472]{1,0:T(8,128)(2,1)})) %all-reduce.5.cloned.1.call-update) | async-done | bytes 1638416 | tf_op jit(solution)/shard_map/psum | solution.py:292
  (198 shorter events, 78.9 us)
Async XLA Ops:
  7.2 83.5 %all-gather.8.cloned.1.call-start = ((), (), s32[]{:S(2)}) async-start(), calls=%async_computation.7 | async-start | bytes 9469952 | tf_op jit(solution)/shard_map/all_gather | solution.py:101
  13.0 194.0 %all-gather.6.cloned.1.call-start = ((), (), s32[]{:S(2)}) async-start(), calls=%async_computation.3 | async-start | bytes 9437184 | tf_op jit(solution)/shard_map/all_gather | solution.py:131
  14.3 99.3 %copy-start.40 = (f32[256]{0:T(256)}, f32[256]{0:T(256)S(1)}, u32[]{:S(2)}) copy-start(f32[256]{0:T(256)S(1)} %add_rsqrt_fusion.1) | copy-start | bytes 3076
  15.1 95.1 %copy-start.33 = (f32[256,32]{0,1:T(8,128)}, f32[256,32]{0,1:T(8,128)S(1)}, u32[]{:S(2)}) copy-start(f32[256,32]{0,1:T(8,128)S(1)} %get-tuple-element.59) | copy-start | bytes 98308
  97.5 16.1 %copy-start.36 = (f32[1024]{0:T(1024)}, f32[1024]{0:T(1024)S(1)}, u32[]{:S(2)}) copy-start(f32[1024]{0:T(1024)S(1)} %reshape.650) | copy-start | bytes 12292
  97.5 7.9 copy-start.9
  110.6 116.0 %copy-start.21 = (bf16[256,16,32]{0,2,1:T(8,128)(2,1)}, bf16[256,16,32]{0,2,1:T(8,128)(2,1)S(1)}, u32[]{:S(2)}) copy-start(bf16[256,16,32]{0,2,1:T(8,128)(2,1)S(1)} %get-tuple-element.41) | copy-start | bytes 786436
  110.6 116.0 %copy-start.23 = (bf16[256,16,32]{0,2,1:T(8,128)(2,1)}, bf16[256,16,32]{0,2,1:T(8,128)(2,1)S(1)}, u32[]{:S(2)}) copy-start(bf16[256,16,32]{0,2,1:T(8,128)(2,1)S(1)} %get-tuple-element.42) | copy-start | bytes 786436
  111.5 5.8 copy-start.32
  117.3 203.7 %all-gather.10.cloned.1.call-start = ((), (), s32[]{:S(2)}) async-start(), calls=%async_computation.8 | async-start | bytes 18382848 | tf_op jit(solution)/shard_map/all_gather | solution.py:110
  120.0 434.4 %reduce-scatter.4.cloned.1.call-start = ((), (), s32[]{:S(2)}) async-start(), calls=%async_computation.4 | async-start | bytes 9437184 | tf_op jit(solution)/shard_map/reduce_scatter | solution.py:234
  121.5 243.4 %copy-start.45 = (pred[256]{0:T(512)(128)(4,1)}, pred[256]{0:T(512)(128)(4,1)S(1)}, u32[]{:S(2)}) copy-start(pred[256]{0:T(512)(128)(4,1)S(1)} %fusion.69) | copy-start | bytes 772
  122.6 242.3 %copy-start.38 = (f32[1024]{0:T(1024)}, f32[1024]{0:T(1024)S(1)}, u32[]{:S(2)}) copy-start(f32[1024]{0:T(1024)S(1)} %reshape.651) | copy-start | bytes 12292
  298.4 66.5 %copy-start.4 = (f32[1,256,1024]{2,1,0:T(8,128)}, f32[1,256,1024]{2,1,0:T(8,128)S(1)}, u32[]{:S(2)}) copy-start(f32[1,256,1024]{2,1,0:T(8,128)S(1)} %get-tuple-element.63) | copy-start | bytes 3145732
  298.4 66.5 %copy-start.42 = (f32[256]{0:T(256)}, f32[256]{0:T(256)S(1)}, u32[]{:S(2)}) copy-start(f32[256]{0:T(256)S(1)} %add_rsqrt_fusion) | copy-start | bytes 3076
  344.3 6.1 copy-start.13
  344.3 9.4 %slice-start.2 = ((s8[5767168]{0:T(1024)(128)(4,1)}), s8[4194304]{0:T(1024)(128)(4,1)S(1)}, s32[]{:S(2)}) async-start(s8[5767168]{0:T(1024)(128)(4,1)} %bitcast.209), calls=%async_computation.12 | async-start | bytes 8388608
  350.5 12.5 %slice-start.4 = ((s8[5767168]{0:T(1024)(128)(4,1)}), s8[4194304]{0:T(1024)(128)(4,1)S(1)}, s32[]{:S(2)}) async-start(s8[5767168]{0:T(1024)(128)(4,1)} %bitcast.212), calls=%async_computation.14 | async-start | bytes 8388608
  353.8 9.2 slice-start.5
  410.8 27.7 %copy-start.22 = (bf16[256,16,32]{0,2,1:T(8,128)(2,1)S(1)}, bf16[256,16,32]{0,2,1:T(8,128)(2,1)}, u32[]{:S(2)}) copy-start(bf16[256,16,32]{0,2,1:T(8,128)(2,1)} %copy-done.21) | copy-start | bytes 786436
  410.8 27.7 %copy-start.24 = (bf16[256,16,32]{0,2,1:T(8,128)(2,1)S(1)}, bf16[256,16,32]{0,2,1:T(8,128)(2,1)}, u32[]{:S(2)}) copy-start(bf16[256,16,32]{0,2,1:T(8,128)(2,1)} %copy-done.23) | copy-start | bytes 786436
  464.0 199.3 %reduce-scatter.6.cloned.1.call-start = ((), (), s32[]{:S(2)}) async-start(), calls=%async_computation.5 | async-start | bytes 7241728 | tf_op jit(solution)/shard_map/reduce_scatter | solution.py:291
  478.1 82.0 %copy-start.34 = (f32[256,32]{0,1:T(8,128)S(1)}, f32[256,32]{0,1:T(8,128)}, u32[]{:S(2)}) copy-start(f32[256,32]{0,1:T(8,128)} %copy-done.33) | copy-start | bytes 98308
  478.1 82.0 %copy-start.35 = (f32[256,32]{0,1:T(8,128)S(1)}, f32[256,32]{0,1:T(8,128)}, u32[]{:S(2)}) copy-start(f32[256,32]{0,1:T(8,128)} %get-tuple-element.57) | copy-start | bytes 98308
  557.1 9.8 %copy-start.8 = (f32[1,256,1024]{2,1,0:T(8,128)}, f32[1,256,1024]{2,1,0:T(8,128)S(1)}, u32[]{:S(2)}) copy-start(f32[1,256,1024]{2,1,0:T(8,128)S(1)} %get-tuple-element.32) | copy-start | bytes 3145732
  572.6 256.0 %reduce-scatter.8.cloned.1.call-start = ((), (), s32[]{:S(2)}) async-start(), calls=%async_computation.6 | async-start | bytes 20611072 | tf_op jit(solution)/shard_map/reduce_scatter | solution.py:200
  575.9 20.8 %copy-start.19 = (bf16[1024,256]{1,0:T(8,128)(2,1)}, bf16[1024,256]{1,0:T(8,128)(2,1)S(1)}, u32[]{:S(2)}) copy-start(bf16[1024,256]{1,0:T(8,128)(2,1)S(1)} %copy.72) | copy-start | bytes 1572868
  581.4 12.1 %copy-start.3 = (f32[1,256,1024]{2,1,0:T(8,128)S(1)}, f32[1,256,1024]{2,1,0:T(8,128)}, u32[]{:S(2)}) copy-start(f32[1,256,1024]{2,1,0:T(8,128)} %copy-done.2) | copy-start | bytes 3145732
  596.8 9.6 %slice-start = ((s8[5767168]{0:T(1024)(128)(4,1)}), s8[4194304]{0:T(1024)(128)(4,1)S(1)}, s32[]{:S(2)}) async-start(s8[5767168]{0:T(1024)(128)(4,1)} %bitcast.193), calls=%async_computation.10 | async-start | bytes 8388608
  619.6 289.3 %all-reduce.5.cloned.1.call-start = ((), (), s32[]{:S(2)}) async-start(), calls=%async_computation.9 | async-start | bytes 3276800 | tf_op jit(solution)/shard_map/psum | solution.py:292
  828.5 5.7 copy-start.7
  828.6 5.7 copy-start.11
  (30 other events, 78.5 us)
Sparse Core Ops, SparseCore 0:
  13.1 77.4 all-gather.7
  117.4 89.5 all-gather.5
  209.4 111.4 all-gather.9
  464.1 90.2 reduce-scatter.3
  572.7 90.6 reduce-scatter.5
  668.3 160.1 reduce-scatter.7
  831.3 77.6 all-reduce.4
where the time goes:
time: 930 us; the launch traced here: 924 us
  waiting for transfers between devices  541 us (58%)
  matrix products  152 us (16%)
  other arithmetic  111 us (12%)
  local copies, waits for them, and re-layouts  104 us (11%)
  between operations  15.1 us (2%)
    reduce_scatter x1, waiting for transfers between devices, body(): lax.psum_scatter(mlp_grads, 'fsdp', scatter_dimension=0, tiled=False)  165 us
    all_gather x1, waiting for transfers between devices, body(): lax.all_gather(jnp.concatenate([key_rot, value_mix], axis=-1), 'ctx', axi...  84.4 us
    reduce_scatter x1, waiting for transfers between devices, body(): lax.psum_scatter(jnp.concatenate([key_part.reshape(total_len, slots, widt...  76.3 us
    all_gather x1, waiting for transfers between devices, body(): attn_all = lax.all_gather(attn_pack, 'fsdp', axis=0, tiled=False)  75.5 us
    psum x1, waiting for transfers between devices, body(): attn_share, mlp_share = lax.psum((attn_share, mlp_share), 'ctx')  73.4 us
    reduce_scatter x1, waiting for transfers between devices, body(): lax.psum_scatter(attn_grads, 'fsdp', scatter_dimension=0, tiled=False)  43.7 us
    sub x1, other arithmetic, body(): raised = jnp.exp(scores - peak)  38.3 us
    convert_element_type x1, other arithmetic, body(): score_gradient = (shares * (prob_back - inner)).astype(jnp.bfloat16)  27.7 us
  transfers between devices with their start and end apart: 7, of which 7 were waited for; matrix products, arithmetic and copies ran while one was open for 18% of the time, Pallas kernels for 0%

commit v1 on v0

--- a/solution.py
+++ b/solution.py
@@ -128,8 +128,14 @@
         .reshape(query.shape)
     )
     value_mix = (0.5 * own_value + 0.5 * first_wide).astype(jnp.bfloat16)
-    kv_all = lax.all_gather(
-        jnp.concatenate([key_rot, value_mix], axis=-1), "ctx", axis=1, tiled=True
+    kv_all = jnp.concatenate(
+        lax.all_to_all(
+            jnp.stack([jnp.concatenate([key_rot, value_mix], axis=-1)] * lax.axis_size("ctx")),
+            "ctx",
+            0,
+            0,
+        ),
+        axis=1,
     )
     key_rows_per_head = kv_all[..., :width].reshape(slots, total_len, head_count, head_dim)
     value_rows_per_head = kv_all[..., width:].reshape(slots, total_len, head_count, head_dim)

time: 930 us -> 966 us (1.039)
  local copies, waits for them, and re-layouts: 104 us -> 121 us
  waiting for transfers between devices: 541 us -> 556 us
    all_to_all x0 -> x1, waiting for transfers between devices: none -> 107 us  [body(): lax.all_to_all(jnp.stack([jnp.concatenate([key_rot, value_mix], axis=-1)]...]
    all_gather x1 -> x0, waiting for transfers between devices: 84.4 us -> none  [body(): lax.all_gather(jnp.concatenate([key_rot, value_mix], axis=-1), 'ctx', axi...]
    all_gather x1, waiting for transfers between devices: 22.5 us -> 0.02 us  [body(): mlp_all = lax.all_gather(mlp_pack, 'fsdp', axis=0, tiled=False)]
    reduce_scatter x1, waiting for transfers between devices: 76.3 us -> 93.8 us  [body(): lax.psum_scatter(jnp.concatenate([key_part.reshape(total_len, slots, widt...]
    all_to_all x0 -> x1, local copies, waits for them, and re-layouts: none -> 11.8 us  [body(): lax.all_to_all(jnp.stack([jnp.concatenate([key_rot, value_mix], axis=-1)]...]
  transfers between devices with their start and end apart: 7 -> 7, of which waited for: 7 -> 6; matrix products, arithmetic and copies ran while one was open for 18% -> 22% of each run, Pallas kernels for 0% -> 0%
where the time goes in v1:
time: 966 us; the launch traced here: 958 us
  waiting for transfers between devices  556 us (58%)
  matrix products  152 us (16%)
  local copies, waits for them, and re-layouts  121 us (13%)
  other arithmetic  109 us (11%)
  between operations  15.1 us (2%)
    reduce_scatter x1, waiting for transfers between devices, body(): lax.psum_scatter(mlp_grads, 'fsdp', scatter_dimension=0, tiled=False)  165 us
    all_to_all x1, waiting for transfers between devices, body(): lax.all_to_all(jnp.stack([jnp.concatenate([key_rot, value_mix], axis=-1)]...  107 us
    reduce_scatter x1, waiting for transfers between devices, body(): lax.psum_scatter(jnp.concatenate([key_part.reshape(total_len, slots, widt...  93.8 us
    psum x1, waiting for transfers between devices, body(): attn_share, mlp_share = lax.psum((attn_share, mlp_share), 'ctx')  73.3 us
    all_gather x1, waiting for transfers between devices, body(): attn_all = lax.all_gather(attn_pack, 'fsdp', axis=0, tiled=False)  72.9 us
    reduce_scatter x1, waiting for transfers between devices, body(): lax.psum_scatter(attn_grads, 'fsdp', scatter_dimension=0, tiled=False)  43.8 us
    sub x1, other arithmetic, body(): raised = jnp.exp(scores - peak)  37.9 us
    convert_element_type x1, other arithmetic, body(): score_gradient = (shares * (prob_back - inner)).astype(jnp.bfloat16)  27.7 us
  transfers between devices with their start and end apart: 7, of which 6 were waited for; matrix products, arithmetic and copies ran while one was open for 22% of the time, Pallas kernels for 0%

profile of v1, /device:TPU:0, one launch (start us, length us, event | category | flops | bytes accessed | tf_op | source)
XLA Modules:
  0.0 958.5 jit_solution(2105315791368935020)
XLA Ops:
  17.8 72.9 %all-gather.5.cloned.1.call-done = bf16[4352,1024]{1,0:T(8,128)(2,1)} async-done(((bf16[272,1024]{1,0:T(8,128)(2,1)}), bf16[4352,1024]{1,0:T(8,128)(2,1)}) %all-gather.5.cloned.1.call-update) | async-done | bytes 8912912 | tf_op jit(solution)/shard_map/all_gather | solution.py:101
  91.7 5.8 fusion.81
  121.4 5.1 all-to-all-start
  129.1 107.2 %all-to-all-done = bf16[8,1,256,2048]{2,3,1,0:T(8,128)(2,1)} async-done(((bf16[8,1,256,2048]{2,3,1,0:T(8,128)(2,1)}), bf16[8,1,256,2048]{2,3,1,0:T(8,128)(2,1)}, u32[]{:S(2)}, u32[]{:S(2)}) %all-to-all-start) | async-done | bytes 8388640 | tf_op jit(solution)/shard_map/all_to_all | solution.py:132
  236.3 11.8 %copy.87 = bf16[8,1,256,2048]{3,2,0,1:T(8,128)(2,1)} copy(bf16[8,1,256,2048]{2,3,1,0:T(8,128)(2,1)} %all-to-all-done) | data formatting | bytes 16777216 | tf_op jit(solution)/shard_map/all_to_all | solution.py:132
  248.1 5.9 fusion.82
  254.1 6.5 copy.90
  260.6 6.6 copy.88
  267.2 16.1 %fusion.55 = f32[16,256,2048]{2,1,0:T(8,128)} fusion(bf16[2048,16,64]{0,2,1:T(8,128)(2,1)} %bitcast.193, bf16[256,16,32]{0,2,1:T(8,128)(2,1)S(1)} %copy-done.23, bf16[256,16,32]{0,2,1:T(8,128)(2,1)S(1)} %get-tuple-element.41), kind=kOutput, calls=%fused_computation.109 | convolution fusion | flops 1074790400 | bytes 38273024 | tf_op jit(solution)/shard_map/biuv,bfuv->buif/dot_general | solution.py:143
  283.3 37.9 %fusion.86 = (f32[16,256]{1,0:T(8,128)S(1)}, f32[16,256,2048]{2,1,0:T(8,128)}) fusion(f32[16,256,2048]{2,1,0:T(8,128)} %fusion.55, pred[256,2048]{1,0:T(8,128)(4,1)S(1)} %fusion.14), kind=kOutput, calls=%fused_computation.157 | output fusion | flops 50333696 | bytes 67649536 | tf_op jit(solution)/shard_map/sub | solution.py:153
  321.2 15.7 %fusion.24 = bf16[16,64,256]{2,1,0:T(8,128)(2,1)} fusion(bf16[2048,16,64]{0,2,1:T(8,128)(2,1)} %bitcast.228, f32[16,256,2048]{2,1,0:T(8,128)} %get-tuple-element.61, f32[16,256]{1,0:T(8,128)S(1)} %get-tuple-element.60), kind=kOutput, calls=%fused_computation.57 | convolution fusion | flops 1090781184 | bytes 38289408 | tf_op jit(solution)/shard_map/ytjo,yotv->yjtv/dot_general | solution.py:157
  339.0 11.6 %fusion.80 = (bf16[16,64,2816]{2,1,0:T(8,128)(2,1)}, bf16[16,64,2816]{2,1,0:T(8,128)(2,1)}, bf16[16,64,2816]{2,1,0:T(8,128)(2,1)}) fusion(bf16[16,64,8448]{2,1,0:T(8,128)(2,1)} %bitcast.205), kind=kLoop, calls=%fused_computation.151 | loop fusion | bytes 34603008 | tf_op jit(solution)/shard_map/slice | solution.py:114
  350.7 12.1 %reshape_reshape.7 = bf16[2816,1024]{1,0:T(8,128)(2,1)} reshape(bf16[16,64,2816]{2,1,0:T(8,128)(2,1)} %get-tuple-element.20) | data formatting | bytes 11534336 | tf_op jit(solution)/shard_map/reshape;reshape | solution.py:114
  362.8 6.1 fusion.48
  372.2 7.5 multiply_convert_fusion.2
  385.7 14.3 %fusion.11 = bf16[16,64,2048]{2,1,0:T(8,128)(2,1)} fusion(bf16[256,16,64]{0,2,1:T(8,128)(2,1)S(1)} %bitcast.236, f32[16,256,2048]{2,1,0:T(8,128)} %get-tuple-element.61, f32[16,256]{1,0:T(8,128)S(1)} %get-tuple-element.60), kind=kOutput, calls=%fused_computation.23 | convolution fusion | flops 1092616192 | bytes 38289408 | tf_op jit(solution)/shard_map/xtfk,xfty->kxty/dot_general | solution.py:234
  400.1 22.7 %multiply_reduce_fusion = (f32[16,256]{1,0:T(8,128)S(1)}, f32[16,256,2048]{2,1,0:T(8,128)}) fusion(f32[16,256,2048]{2,1,0:T(8,128)} %get-tuple-element.61, f32[16,256]{1,0:T(8,128)S(1)} %get-tuple-element.60, bf16[256,16,64]{0,2,1:T(8,128)(2,1)S(1)} %bitcast.237, bf16[2048,16,64]{0,2,1:T(8,128)(2,1)} %bitcast.229), kind=kOutput, calls=%fused_computation.2 | convolution fusion | flops 1098903552 | bytes 71860224 | tf_op jit(solution)/shard_map/biuv,bfuv->buif/dot_general | solution.py:211
  422.8 6.4 copy.93
  429.2 27.7 %multiply_convert_fusion = bf16[16,256,2048]{2,1,0:T(8,128)(2,1)} fusion(f32[16,256,2048]{2,1,0:T(8,128)} %get-tuple-element.66, f32[16,256]{1,0:T(8,128)S(1)} %get-tuple-element.65, f32[16,256,2048]{2,1,0:T(8,128)} %get-tuple-element.61, f32[16,256]{1,0:T(8,128)S(1)} %get-tuple-element.60), kind=kLoop, calls=%fused_computation.1 | loop fusion | flops 33554432 | bytes 83918848 | tf_op jit(solution)/shard_map/convert_element_type | solution.py:218
  457.0 10.8 %multiply_convert_fusion.1 = bf16[16,64,2048]{2,1,0:T(8,128)(2,1)} fusion(bf16[16,256,2048]{2,1,0:T(8,128)(2,1)} %multiply_convert_fusion, bf16[256,16,32]{0,2,1:T(8,128)(2,1)S(1)} %copy-done.24, bf16[256,16,32]{0,2,1:T(8,128)(2,1)S(1)} %copy-done.22), kind=kOutput, calls=%fused_computation.14 | convolution fusion | flops 1078984704 | bytes 21495808 | tf_op jit(solution)/shard_map/xtfk,xfty->kxty/dot_general | solution.py:226
  467.7 6.4 copy.92
  474.2 8.2 pad_maximum_fusion.1
  482.6 13.2 %fusion.17 = f32[1,256,16,64]{1,3,2,0:T(8,128)} fusion(bf16[2048,16,64]{0,2,1:T(8,128)(2,1)} %bitcast.194, bf16[16,256,2048]{2,1,0:T(8,128)(2,1)} %multiply_convert_fusion), kind=kOutput, calls=%fused_computation.46 | convolution fusion | flops 1074003968 | bytes 22020096 | tf_op jit(solution)/shard_map/ytjo,yotv->yjtv/dot_general | solution.py:220
  495.8 93.8 %reduce-scatter.4.cloned.1.call-done = bf16[256,1,2048]{2,0,1:T(8,128)(2,1)} async-done(((bf16[2048,1,2048]{2,0,1:T(8,128)(2,1)}), bf16[256,1,2048]{2,0,1:T(8,128)(2,1)}) %reduce-scatter.4.cloned.1.call-update) | async-done | bytes 1048592 | tf_op jit(solution)/shard_map/reduce_scatter | solution.py:240
  611.2 5.4 convolution_convert_fusion
  616.6 12.1 %reshape_reshape.8 = bf16[16,64,2816]{2,1,0:T(8,128)(2,1)} reshape(bf16[2816,1024]{1,0:T(8,128)(2,1)} %convolution_convert_fusion) | data formatting | bytes 11534336 | tf_op jit(solution)/shard_map/reshape;reshape | solution.py:201
  636.1 5.4 convolution_convert_fusion.2
  641.5 13.3 %pad_maximum_fusion = bf16[16,64,9472]{2,1,0:T(8,128)(2,1)} fusion(bf16[16,64,1024]{2,1,0:T(8,128)(2,1)} %convolution_convert_fusion.3, bf16[16,64,2816]{2,1,0:T(8,128)(2,1)S(1)} %bitcast.198, bf16[16,64,2816]{2,1,0:T(8,128)(2,1)} %convolution_convert_fusion.1, bf16[16,64,2816]{2,1,0:T(8,128)(2,1)} %convolution_convert_fusion.2), kind=kLoop, calls=%fused_computation.6 | loop fusion | flops 77594624 | bytes 38797312 | tf_op jit(solution)/shard_map/concatenate | solution.py:197
  654.9 43.8 %reduce-scatter.6.cloned.1.call-done = bf16[1,208,1024]{2,1,0:T(8,128)(2,1)} async-done(((bf16[16,208,1024]{2,1,0:T(8,128)(2,1)}), bf16[1,208,1024]{2,1,0:T(8,128)(2,1)}) %reduce-scatter.6.cloned.1.call-update) | async-done | bytes 426000 | tf_op jit(solution)/shard_map/reduce_scatter | solution.py:297
  698.6 164.8 %reduce-scatter.8.cloned.1.call-done = bf16[1,64,9472]{2,1,0:T(8,128)(2,1)} async-done(((bf16[16,64,9472]{2,1,0:T(8,128)(2,1)}), bf16[1,64,9472]{2,1,0:T(8,128)(2,1)}) %reduce-scatter.8.cloned.1.call-update) | async-done | bytes 1212432 | tf_op jit(solution)/shard_map/reduce_scatter | solution.py:206
  863.5 5.7 fusion.23
  870.5 73.3 %all-reduce.5.cloned.1.call-done = (bf16[208,1024]{1,0:T(8,128)(2,1)}, bf16[64,9472]{1,0:T(8,128)(2,1)}) async-done(((bf16[208,1024]{1,0:T(8,128)(2,1)}, bf16[64,9472]{1,0:T(8,128)(2,1)}), (bf16[208,1024]{1,0:T(8,128)(2,1)}, bf16[64,9472]{1,0:T(8,128)(2,1)})) %all-reduce.5.cloned.1.call-update) | async-done | bytes 1638416 | tf_op jit(solution)/shard_map/psum | solution.py:298
  (198 shorter events, 87.2 us)
Async XLA Ops:
  7.2 9.6 %copy-start.9 = (bf16[1,256,1024]{2,1,0:T(8,128)(2,1)S(1)}, bf16[1,256,1024]{2,1,0:T(8,128)(2,1)}, u32[]{:S(2)}) copy-start(bf16[1,256,1024]{2,1,0:T(8,128)(2,1)} %param.14) | copy-start | bytes 1572868
  7.2 83.5 %all-gather.5.cloned.1.call-start = ((), (), s32[]{:S(2)}) async-start(), calls=%async_computation.7 | async-start | bytes 9469952 | tf_op jit(solution)/shard_map/all_gather | solution.py:101
  13.1 326.0 %all-gather.7.cloned.1.call-start = ((), (), s32[]{:S(2)}) async-start(), calls=%async_computation.8 | async-start | bytes 18382848 | tf_op jit(solution)/shard_map/all_gather | solution.py:110
  17.0 95.4 %copy-start.39 = (f32[256]{0:T(256)}, f32[256]{0:T(256)S(1)}, u32[]{:S(2)}) copy-start(f32[256]{0:T(256)S(1)} %add_rsqrt_fusion.1) | copy-start | bytes 3076
  17.8 92.5 %copy-start.32 = (f32[256,32]{0,1:T(8,128)}, f32[256,32]{0,1:T(8,128)S(1)}, u32[]{:S(2)}) copy-start(f32[256,32]{0,1:T(8,128)S(1)} %get-tuple-element.59) | copy-start | bytes 98308
  91.7 20.7 %copy-start.35 = (f32[1024]{0:T(1024)}, f32[1024]{0:T(1024)S(1)}, u32[]{:S(2)}) copy-start(f32[1024]{0:T(1024)S(1)} %reshape.657) | copy-start | bytes 12292
  111.4 155.8 %copy-start.21 = (bf16[256,16,32]{0,2,1:T(8,128)(2,1)}, bf16[256,16,32]{0,2,1:T(8,128)(2,1)S(1)}, u32[]{:S(2)}) copy-start(bf16[256,16,32]{0,2,1:T(8,128)(2,1)S(1)} %get-tuple-element.41) | copy-start | bytes 786436
  121.4 115.0 %all-to-all-start = ((bf16[8,1,256,2048]{2,3,1,0:T(8,128)(2,1)}), bf16[8,1,256,2048]{2,3,1,0:T(8,128)(2,1)}, u32[]{:S(2)}, u32[]{:S(2)}) async-start(bf16[8,1,256,2048]{2,3,1,0:T(8,128)(2,1)} %stack.2), calls=%async_computation | async-start | bytes 16777216 | tf_op jit(solution)/shard_map/all_to_all | solution.py:132
  126.5 463.1 %reduce-scatter.4.cloned.1.call-start = ((), (), s32[]{:S(2)}) async-start(), calls=%async_computation.4 | async-start | bytes 9437184 | tf_op jit(solution)/shard_map/reduce_scatter | solution.py:240
  128.0 255.3 %copy-start.44 = (pred[256]{0:T(512)(128)(4,1)}, pred[256]{0:T(512)(128)(4,1)S(1)}, u32[]{:S(2)}) copy-start(pred[256]{0:T(512)(128)(4,1)S(1)} %fusion.69) | copy-start | bytes 772
  129.1 254.2 %copy-start.37 = (f32[1024]{0:T(1024)}, f32[1024]{0:T(1024)S(1)}, u32[]{:S(2)}) copy-start(f32[1024]{0:T(1024)S(1)} %reshape.658) | copy-start | bytes 12292
  260.6 6.6 copy-start.23
  339.0 44.3 %copy-start.4 = (f32[1,256,1024]{2,1,0:T(8,128)}, f32[1,256,1024]{2,1,0:T(8,128)S(1)}, u32[]{:S(2)}) copy-start(f32[1,256,1024]{2,1,0:T(8,128)S(1)} %get-tuple-element.63) | copy-start | bytes 3145732
  339.0 44.3 %copy-start.41 = (f32[256]{0:T(256)}, f32[256]{0:T(256)S(1)}, u32[]{:S(2)}) copy-start(f32[256]{0:T(256)S(1)} %add_rsqrt_fusion) | copy-start | bytes 3076
  362.8 6.1 copy-start.13
  362.8 9.4 slice-start.2
  368.9 12.5 %slice-start.4 = ((s8[5767168]{0:T(1024)(128)(4,1)}), s8[4194304]{0:T(1024)(128)(4,1)S(1)}, s32[]{:S(2)}) async-start(s8[5767168]{0:T(1024)(128)(4,1)} %bitcast.216), calls=%async_computation.14 | async-start | bytes 8388608
  372.2 9.2 slice-start.5
  429.2 27.7 %copy-start.22 = (bf16[256,16,32]{0,2,1:T(8,128)(2,1)S(1)}, bf16[256,16,32]{0,2,1:T(8,128)(2,1)}, u32[]{:S(2)}) copy-start(bf16[256,16,32]{0,2,1:T(8,128)(2,1)} %copy-done.21) | copy-start | bytes 786436
  429.2 27.8 %copy-start.24 = (bf16[256,16,32]{0,2,1:T(8,128)(2,1)S(1)}, bf16[256,16,32]{0,2,1:T(8,128)(2,1)}, u32[]{:S(2)}) copy-start(bf16[256,16,32]{0,2,1:T(8,128)(2,1)} %get-tuple-element.42) | copy-start | bytes 786436
  482.4 216.2 %reduce-scatter.6.cloned.1.call-start = ((), (), s32[]{:S(2)}) async-start(), calls=%async_computation.5 | async-start | bytes 7241728 | tf_op jit(solution)/shard_map/reduce_scatter | solution.py:297
  495.8 99.5 %copy-start.33 = (f32[256,32]{0,1:T(8,128)S(1)}, f32[256,32]{0,1:T(8,128)}, u32[]{:S(2)}) copy-start(f32[256,32]{0,1:T(8,128)} %copy-done.32) | copy-start | bytes 98308
  495.8 99.5 %copy-start.34 = (f32[256,32]{0,1:T(8,128)S(1)}, f32[256,32]{0,1:T(8,128)}, u32[]{:S(2)}) copy-start(f32[256,32]{0,1:T(8,128)} %get-tuple-element.57) | copy-start | bytes 98308
  592.3 9.8 %copy-start.8 = (f32[1,256,1024]{2,1,0:T(8,128)}, f32[1,256,1024]{2,1,0:T(8,128)S(1)}, u32[]{:S(2)}) copy-start(f32[1,256,1024]{2,1,0:T(8,128)S(1)} %get-tuple-element.32) | copy-start | bytes 3145732
  607.8 255.6 %reduce-scatter.8.cloned.1.call-start = ((), (), s32[]{:S(2)}) async-start(), calls=%async_computation.6 | async-start | bytes 20611072 | tf_op jit(solution)/shard_map/reduce_scatter | solution.py:206
  611.1 20.8 %copy-start.19 = (bf16[1024,256]{1,0:T(8,128)(2,1)}, bf16[1024,256]{1,0:T(8,128)(2,1)S(1)}, u32[]{:S(2)}) copy-start(bf16[1024,256]{1,0:T(8,128)(2,1)S(1)} %copy.99) | copy-start | bytes 1572868
  616.6 12.1 %copy-start.3 = (f32[1,256,1024]{2,1,0:T(8,128)S(1)}, f32[1,256,1024]{2,1,0:T(8,128)}, u32[]{:S(2)}) copy-start(f32[1,256,1024]{2,1,0:T(8,128)} %copy-done.2) | copy-start | bytes 3145732
  631.9 9.6 %slice-start = ((s8[5767168]{0:T(1024)(128)(4,1)}), s8[4194304]{0:T(1024)(128)(4,1)S(1)}, s32[]{:S(2)}) async-start(s8[5767168]{0:T(1024)(128)(4,1)} %bitcast.197), calls=%async_computation.10 | async-start | bytes 8388608
  636.1 5.4 slice-start.1
  654.8 289.0 %all-reduce.5.cloned.1.call-start = ((), (), s32[]{:S(2)}) async-start(), calls=%async_computation.9 | async-start | bytes 3276800 | tf_op jit(solution)/shard_map/psum | solution.py:298
  863.4 5.7 copy-start.7
  863.4 5.7 copy-start.11
  (29 other events, 75.7 us)
Sparse Core Ops, SparseCore 0:
  13.2 77.4 all-gather.4
  93.1 190.3 all-gather.6
  482.6 106.9 reduce-scatter.3
  607.9 90.6 reduce-scatter.5
  703.6 159.8 reduce-scatter.7
  866.0 77.7 all-reduce.4
